TPU v7x, 32 devices: a whole 2x2x4 slice. The times are simulated.
32 devices in a mesh: param: 4 (over x, core), space: 8 (over z, y).
Axes of the slice: x: 2, y: 2, z: 4, core: 2. Of those that a mesh axis runs over, the one named last changes fastest.
Arguments:
- fine_state: bfloat16 [16, 16, 64, 512], P('space', None, None, 'param'), may hold values from -6 to 6
- fine_tangent: bfloat16 [16, 16, 64, 512], P('space', None, None, 'param'), may hold values from -6 to 6
- down_weight: float32 [8, 512, 1024], P(None, 'space', 'param'), may hold values from -0.09375 to 0.09375
- conv_weight: float32 [27, 1024, 1024], P(None, 'space', 'param'), may hold values from -0.0390625 to 0.0390625
- up_weight: float32 [8, 1024, 512], P(None, 'space', 'param'), may hold values from -0.1875 to 0.1875
Outputs:
- state_out: bfloat16 [16, 16, 64, 512], P('space', None, None, 'param')
- tangent_out: bfloat16 [16, 16, 64, 512], P('space', None, None, 'param')
All inputs are finite; a program needn't handle non-finite values.
Results may differ from a plain program's by a relative error of at most 0.0075.
Values may be sent and summed in bfloat16 or wider, within the bound.
No kernel may reach another device: no remote copies, remote signals or barrier semaphores. Data moves between devices by JAX's collectives and lax.ppermute only.
A program may use at most 128 MiB of HBM per device.

v0:
```python
import jax
import jax.numpy as jnp
from jax import lax
from jax.sharding import PartitionSpec as P


def padded(block, sides, width):
    for axis, dim in sides:
        count = lax.axis_size(axis)
        forward = [(i, i + 1) for i in range(count - 1)]
        backward = [(target, source) for source, target in forward]
        low = lax.ppermute(
            lax.slice_in_dim(block, block.shape[dim] - width, None, axis=dim), axis, forward
        )
        high = lax.ppermute(lax.slice_in_dim(block, 0, width, axis=dim), axis, backward)
        block = jnp.concatenate([low, block, high], axis=dim)
    return block


def partner(block, axis, apart):
    count = lax.axis_size(axis)
    route = []
    for low in range(count):
        high = low | 1 << apart
        if high != low and high < count:
            route += [(low, high), (high, low)]
    return lax.ppermute(block, axis, route)


def silu_pair(primal, tangent):
    sigma = jax.nn.sigmoid(primal)
    return (primal * sigma, sigma * (1.0 + primal * (1.0 - sigma)) * tangent)


def cube_block(source, kernel, planes):
    span_y = source.shape[2] - 2
    span_x = source.shape[3] - 2
    width = source.shape[4]
    result = None
    for tap_z in range(3):
        for tap_y in range(3):
            window = jnp.stack(
                [
                    source[
                        :, tap_z : tap_z + planes, tap_y : tap_y + span_y, tap_x : tap_x + span_x, :
                    ]
                    for tap_x in range(3)
                ],
                axis=4,
            )
            window = window.reshape(-1, 3 * width)
            first_tap = 9 * tap_z + 3 * tap_y
            weights = kernel[first_tap : first_tap + 3].reshape(3 * width, kernel.shape[2])
            term = jnp.dot(window, weights, preferred_element_type=jnp.float32)
            result = term if result is None else result + term
    return result


def local(fine_state, fine_tangent, down_weight, conv_weight, up_weight):
    planes = fine_state.shape[0] // 2
    span_y = fine_state.shape[1] // 2
    span_x = fine_state.shape[2] // 2
    cells = planes * span_y * span_x
    state_full, tangent_full = (
        lax.all_gather(fine_state, "param", axis=3, tiled=True),
        lax.all_gather(fine_tangent, "param", axis=3, tiled=True),
    )
    wide_fine = state_full.shape[3]
    paired = jnp.stack([state_full, tangent_full], axis=0)
    patches = (
        paired.reshape(2, planes, 2, span_y, 2, span_x, 2, wide_fine)
        .transpose(0, 1, 3, 5, 2, 4, 6, 7)
        .reshape(2 * cells, 8, wide_fine)
    )
    down_kernel = down_weight.astype(jnp.bfloat16)
    up_kernel = up_weight.astype(jnp.bfloat16)
    cube_kernel = conv_weight.astype(jnp.bfloat16)
    coarse_local = down_weight.shape[2]
    fine_local = up_weight.shape[2]
    portion = lax.all_gather(down_kernel, "space", axis=1, tiled=True)
    width = portion.shape[1]
    columns = patches.reshape(2 * cells, 8 * width)
    first_pre = jnp.dot(
        columns, portion.reshape(8 * width, portion.shape[2]), preferred_element_type=jnp.float32
    )
    first_pre = first_pre.reshape(2, cells, coarse_local)
    first_val, first_dir = silu_pair(first_pre[0], first_pre[1])
    first_round = jnp.stack(
        [first_val.astype(jnp.bfloat16), first_dir.astype(jnp.bfloat16)], axis=0
    )
    first_stack = first_round.reshape(2, planes, span_y, span_x, coarse_local)
    haloed = padded(first_stack, (("space", 1),), 1)
    every_channel = lax.all_gather(haloed, "param", axis=4, tiled=True)
    position = lax.axis_index("space")
    levels = lax.axis_size("space").bit_length() - 1
    wide_coarse = every_channel.shape[4]
    block_kernel = cube_kernel
    for bit in range(levels - 1):
        partner_block = partner(block_kernel, "space", bit)
        upper = position >> bit & 1
        block_kernel = jnp.where(
            upper == 1,
            jnp.concatenate([partner_block, block_kernel], axis=1),
            jnp.concatenate([block_kernel, partner_block], axis=1),
        )
    half_index = position >> levels - 1
    own_half = lax.dynamic_slice_in_dim(
        every_channel, half_index * (wide_coarse // 2), wide_coarse // 2, 4
    )
    send_half = lax.dynamic_slice_in_dim(
        every_channel, (1 - half_index) * (wide_coarse // 2), wide_coarse // 2, 4
    )
    other_half = partner(send_half, "space", levels - 1)
    own_padded = jnp.pad(own_half, ((0, 0), (0, 0), (1, 1), (1, 1), (0, 0)))
    other_padded = jnp.pad(other_half, ((0, 0), (0, 0), (1, 1), (1, 1), (0, 0)))
    own_sum = cube_block(own_padded, block_kernel, planes)
    other_sum = cube_block(other_padded, block_kernel, planes)
    returned = partner(other_sum.astype(jnp.bfloat16), "space", levels - 1).astype(other_sum.dtype)
    second_pre = (own_sum + returned).reshape(2, cells, coarse_local)
    second_val, second_dir = silu_pair(second_pre[0], second_pre[1])
    second_val = second_val + first_round[0].astype(jnp.float32)
    second_dir = second_dir + first_round[1].astype(jnp.float32)
    top_stack = jnp.stack(
        [second_val.astype(jnp.bfloat16), second_dir.astype(jnp.bfloat16)], axis=0
    )
    top_full = lax.all_gather(top_stack, "param", axis=2, tiled=True)
    top_rows = top_full.reshape(2 * cells, top_full.shape[2])
    portion = lax.all_gather(up_kernel, "space", axis=1, tiled=True)
    width = portion.shape[1]
    columns = top_rows
    product = jnp.dot(
        columns,
        portion.transpose(1, 0, 2).reshape(width, 8 * fine_local),
        preferred_element_type=jnp.float32,
    )
    shaped = product.reshape(2, planes, span_y, span_x, 2, 2, 2, fine_local).transpose(
        0, 1, 4, 2, 5, 3, 6, 7
    )
    outputs = shaped.reshape(2, 2 * planes, 2 * span_y, 2 * span_x, fine_local).astype(jnp.bfloat16)
    return (outputs[0], outputs[1])


def solution(mesh):
    in_specs = (
        P("space", None, None, "param"),
        P("space", None, None, "param"),
        P(None, "space", "param"),
        P(None, "space", "param"),
        P(None, "space", "param"),
    )
    out_specs = (P("space", None, None, "param"), P("space", None, None, "param"))
    return jax.shard_map(local, mesh=mesh, in_specs=in_specs, out_specs=out_specs, check_vma=False)
```

profile of v0, /device:TPU:0, one launch (start us, length us, event | category | flops | bytes accessed | tf_op | source)
XLA Modules:
  0.0 400.6 jit_solution(16361517730919954494)
XLA Ops:
  8.7 1.8 convert_element_type.46
  10.5 3.5 convert_element_type.49
  14.0 3.0 collective-permute-start.2
  17.0 18.1 %all-gather.9.cloned.1.call-done = bf16[2,16,64,512]{3,2,1,0:T(8,128)(2,1)} async-done(((bf16[2,16,64,128]{3,2,1,0:T(8,128)(2,1)}), bf16[2,16,64,512]{3,2,1,0:T(8,128)(2,1)}) %all-gather.9.cloned.1.call-update) | async-done | bytes 2097168 | tf_op jit(solution)/shard_map/all_gather | solution.py:66
  35.1 2.7 stack.244
  37.8 21.6 %all-gather.7.cloned.1.call-done = bf16[2,16,64,512]{3,2,1,0:T(8,128)(2,1)} async-done(((bf16[2,16,64,128]{3,2,1,0:T(8,128)(2,1)}), bf16[2,16,64,512]{3,2,1,0:T(8,128)(2,1)}) %all-gather.7.cloned.1.call-update) | async-done | bytes 2097168 | tf_op jit(solution)/shard_map/all_gather | solution.py:65
  59.5 4.1 %stack.243 = bf16[1,1,2,8,2,32,2,512]{7,6,5,4,3,2,1,0:T(2,128)(2,1)} reshape(bf16[2,16,64,512]{3,2,1,0:T(8,128)(2,1)} %all-gather.7.cloned.1.call-done) | data formatting | bytes 4194304 | tf_op jit(solution)/shard_map/stack | solution.py:69
  63.6 7.8 %copy_bitcast_fusion = bf16[2,1,8,32,2,2,2,512]{7,6,5,4,3,2,0,1:T(2,128)(2,1)} fusion(bf16[1,1,2,8,2,32,2,512]{7,6,5,4,3,2,1,0:T(2,128)(2,1)S(1)} %stack.244, bf16[1,1,2,8,2,32,2,512]{7,6,5,4,3,2,1,0:T(2,128)(2,1)} %stack.243), kind=kLoop, calls=%fused_computation.50 | loop fusion | flops 2097152 | bytes 8388608 | tf_op jit(solution)/shard_map/transpose | solution.py:72
  71.4 7.8 %reshape_reshape.3 = bf16[512,4096]{1,0:T(8,128)(2,1)} reshape(bf16[2,1,8,32,2,2,2,512]{7,6,5,4,3,2,0,1:T(2,128)(2,1)} %copy_bitcast_fusion) | data formatting | bytes 8388608 | tf_op jit(solution)/shard_map/reshape;reshape | solution.py:82
  79.2 32.2 %all-gather.11.cloned.1.call-done = bf16[8,512,256]{2,1,0:T(8,128)(2,1)} async-done(((bf16[8,64,256]{2,1,0:T(8,128)(2,1)}), bf16[8,512,256]{2,1,0:T(8,128)(2,1)}) %all-gather.11.cloned.1.call-update) | async-done | bytes 2097168 | tf_op jit(solution)/shard_map/all_gather | solution.py:80
  111.4 4.1 %fusion.72 = f32[512,256]{1,0:T(8,128)S(1)} fusion(bf16[512,4096]{1,0:T(8,128)(2,1)} %reshape_reshape.3, bf16[4096,256]{1,0:T(8,128)(2,1)} %bitcast.331), kind=kOutput, calls=%fused_computation.162 | convolution fusion | flops 1073741824 | bytes 6815744 | tf_op jit(solution)/shard_map/dot_general | solution.py:83
  117.0 4.6 %collective-permute-start = (bf16[2,1,8,32,256]{4,3,2,0,1:T(8,128)(2,1)S(1)}, bf16[2,1,8,32,256]{4,3,2,0,1:T(8,128)(2,1)S(1)}, u32[]{:S(2)}, u32[]{:S(2)}) collective-permute-start(bf16[2,1,8,32,256]{4,3,2,0,1:T(8,128)(2,1)S(1)} %pad_maximum_fusion.20), channel_id=1, source_target_pairs={{0,1},{1,2},{2,3},{3,4},{4,5},{5,6},{6,7},{8,9},{9,10},{10,11},{11... | collective-permute-start | bytes 786440 | tf_op jit(solution)/shard_map/ppermute | solution.py:12
  121.5 2.4 collective-permute-done.1
  123.9 5.0 %collective-permute-done = bf16[2,1,8,32,256]{4,3,2,0,1:T(8,128)(2,1)S(1)} collective-permute-done((bf16[2,1,8,32,256]{4,3,2,0,1:T(8,128)(2,1)S(1)}, bf16[2,1,8,32,256]{4,3,2,0,1:T(8,128)(2,1)S(1)}, u32[]{:S(2)}, u32[]{:S(2)}) %collective-permute-start) | collective-permute-done | bytes 262176 | tf_op jit(solution)/shard_map/ppermute | solution.py:12
  130.0 4.0 maximum_select_fusion.1
  134.0 2.8 collective-permute-start.3
  136.8 1.9 copy.61
  138.8 99.1 %collective-permute-done.3 = bf16[27,256,256]{2,1,0:T(8,128)(2,1)} collective-permute-done((bf16[27,256,256]{2,1,0:T(8,128)(2,1)S(1)}, bf16[27,256,256]{2,1,0:T(8,128)(2,1)}, u32[]{:S(2)}, u32[]{:S(2)}) %collective-permute-start.3) | collective-permute-done | bytes 3538976 | tf_op jit(solution)/shard_map/ppermute | solution.py:27
  237.9 5.1 %maximum_select_fusion = bf16[27,512,256]{2,1,0:T(8,128)(2,1)S(1)} fusion(bf16[27,256,256]{2,1,0:T(8,128)(2,1)S(1)} %maximum_select_fusion.1, bf16[27,256,256]{2,1,0:T(8,128)(2,1)} %collective-permute-done.3, pred[]{:T(512)S(6)} %eq.6), kind=kLoop, calls=%fused_computation | loop fusion | flops 31850496 | bytes 14155777 | tf_op jit(solution)/shard_map/jit(_where)/select_n | solution.py:101
  243.0 1.9 fusion.70
  245.0 2.3 constant_dynamic-slice_fusion
  247.7 4.1 %fusion.17 = (bf16[2,1,8,32,1,512]{5,3,2,0,4,1:T(8,128)(2,1)S(1)}, bf16[2,1,8,32,1,512]{5,3,2,0,4,1:T(8,128)(2,1)S(1)}, bf16[2,1,8,32,1,512]{5,3,2,0,4,1:T(8,128...) fusion(bf16[2,3,8,32,512]{4,3,2,0,1:T(8,128)(2,1)S(1)} %get-tup, ...), kind=kLoop, calls=%fused_computation.91 | loop fusion | bytes 11534336 | tf_op jit(solution)/shard_map/stack | solution.py:42
  256.2 2.5 collective-permute-start.4
  261.1 1.4 copy.49
  264.9 1.8 copy.47
  278.9 46.7 %collective-permute-done.4 = bf16[2,3,8,32,512]{4,3,2,0,1:T(8,128)(2,1)S(1)} collective-permute-done((bf16[2,3,8,32,512]{4,3,2,0,1:T(8,128)(2,1)S(1)}, bf16[2,3,8,32,512]{4,3,2,0,1:T(8,128)(2,1)S(1)}, u32[]{:S(2)}, u32[]{:S(2)}) %collective-permute-start.4) | collective-permute-done | bytes 1572896 | tf_op jit(solution)/shard_map/ppermute | solution.py:27
  326.5 1.5 copy.60
  331.1 3.9 fusion.41
  345.8 1.6 copy.53
  355.2 11.3 %collective-permute-done.5 = bf16[512,256]{1,0:T(8,128)(2,1)S(1)} collective-permute-done((bf16[512,256]{1,0:T(8,128)(2,1)S(1)}, bf16[512,256]{1,0:T(8,128)(2,1)S(1)}, u32[]{:S(2)}, u32[]{:S(2)}) %collective-permute-start.5) | collective-permute-done | bytes 262176 | tf_op jit(solution)/shard_map/ppermute | solution.py:27
  368.4 19.1 %all-gather.15.cloned.1.call-done = bf16[2,256,1024]{2,1,0:T(8,128)(2,1)} async-done(((bf16[2,256,256]{2,1,0:T(8,128)(2,1)}), bf16[2,256,1024]{2,1,0:T(8,128)(2,1)}) %all-gather.15.cloned.1.call-update) | async-done | bytes 1048592 | tf_op jit(solution)/shard_map/all_gather | solution.py:126
  387.6 3.2 fusion
  (108 shorter events, 52.7 us)
Async XLA Ops:
  7.2 27.9 %all-gather.9.cloned.1.call-start = ((), (), s32[]{:S(2)}) async-start(), calls=%async_computation.1 | async-start | bytes 2621440 | tf_op jit(solution)/shard_map/all_gather | solution.py:66
  7.9 51.6 %all-gather.7.cloned.1.call-start = ((), (), s32[]{:S(2)}) async-start(), calls=%async_computation | async-start | bytes 2621440 | tf_op jit(solution)/shard_map/all_gather | solution.py:65
  8.6 102.7 %all-gather.11.cloned.1.call-start = ((), (), s32[]{:S(2)}) async-start(), calls=%async_computation.2 | async-start | bytes 2359296 | tf_op jit(solution)/shard_map/all_gather | solution.py:80
  10.5 234.5 %all-gather.13.cloned.1.call-start = ((), (), s32[]{:S(2)}) async-start(), calls=%async_computation.3 | async-start | bytes 3932160 | tf_op jit(solution)/shard_map/all_gather | solution.py:93
  14.0 115.9 %collective-permute-start.2 = (bf16[27,128,256]{2,1,0:T(8,128)(2,1)}, bf16[27,128,256]{2,1,0:T(8,128)(2,1)}, u32[]{:S(2)}, u32[]{:S(2)}) collective-permute-start(bf16[27,128,256]{2,1,0:T(8,128)(2,1)} %convert_element_type.49), channel_id=1, source_target_pairs={{0,1},{1,0},{2,3},{3,2},{4,5},{5,4},{6,7},{7,6},{8,9},{9,8},{10,11... | collective-permute-start | bytes 5308424 | tf_op jit(solution)/shard_map/ppermute | solution.py:27
  115.6 13.3 %copy-start.6 = (bf16[256,256]{1,0:T(8,128)(2,1)}, bf16[256,256]{1,0:T(8,128)(2,1)S(1)}, u32[]{:S(2)}) copy-start(bf16[256,256]{1,0:T(8,128)(2,1)S(1)} %get-tuple-element.71) | copy-start | bytes 393220
  115.6 13.3 %copy-start.8 = (bf16[256,256]{1,0:T(8,128)(2,1)}, bf16[256,256]{1,0:T(8,128)(2,1)S(1)}, u32[]{:S(2)}) copy-start(bf16[256,256]{1,0:T(8,128)(2,1)S(1)} %get-tuple-element.72) | copy-start | bytes 393220
  115.7 8.3 %collective-permute-start.1 = (bf16[2,1,8,32,256]{4,3,2,0,1:T(8,128)(2,1)S(1)}, bf16[2,1,8,32,256]{4,3,2,0,1:T(8,128)(2,1)S(1)}, u32[]{:S(2)}, u32[]{:S(2)}) collective-permute-start(bf16[2,1,8,32,256]{4,3,2,0,1:T(8,128)(2,1)S(1)} %pad_maximum_fusion.20), channel_id=1, source_target_pairs={{1,0},{2,1},{3,2},{4,3},{5,4},{6,5},{7,6},{9,8},{10,9},{11,10},{12... | collective-permute-start | bytes 786440 | tf_op jit(solution)/shard_map/ppermute | solution.py:15
  117.0 12.0 %collective-permute-start = (bf16[2,1,8,32,256]{4,3,2,0,1:T(8,128)(2,1)S(1)}, bf16[2,1,8,32,256]{4,3,2,0,1:T(8,128)(2,1)S(1)}, u32[]{:S(2)}, u32[]{:S(2)}) collective-permute-start(bf16[2,1,8,32,256]{4,3,2,0,1:T(8,128)(2,1)S(1)} %pad_maximum_fusion.20), channel_id=1, source_target_pairs={{0,1},{1,2},{2,3},{3,4},{4,5},{5,6},{6,7},{8,9},{9,10},{10,11},{11... | collective-permute-start | bytes 786440 | tf_op jit(solution)/shard_map/ppermute | solution.py:12
  129.9 238.5 %all-gather.17.cloned.1.call-start = ((), (), s32[]{:S(2)}) async-start(), calls=%async_computation.5 | async-start | bytes 2359296 | tf_op jit(solution)/shard_map/all_gather | solution.py:128
  134.0 103.9 %collective-permute-start.3 = (bf16[27,256,256]{2,1,0:T(8,128)(2,1)S(1)}, bf16[27,256,256]{2,1,0:T(8,128)(2,1)}, u32[]{:S(2)}, u32[]{:S(2)}) collective-permute-start(bf16[27,256,256]{2,1,0:T(8,128)(2,1)S(1)} %maximum_select_fusion.1), channel_id=1, source_target_pairs={{0,2},{2,0},{1,3},{3,1},{4,6},{6,4},{5,7},{7,5},{8,10},{10,8},{9,1... | collective-permute-start | bytes 10616840 | tf_op jit(solution)/shard_map/ppermute | solution.py:27
  138.7 248.8 %all-gather.15.cloned.1.call-start = ((), (), s32[]{:S(2)}) async-start(), calls=%async_computation.4 | async-start | bytes 1310720 | tf_op jit(solution)/shard_map/all_gather | solution.py:126
  247.7 4.1 %copy-start.5 = (bf16[2,3,8,32,1024]{4,3,2,0,1:T(8,128)(2,1)S(1)}, bf16[2,3,8,32,1024]{4,3,2,0,1:T(8,128)(2,1)}, u32[]{:S(2)}) copy-start(bf16[2,3,8,32,1024]{4,3,2,0,1:T(8,128)(2,1)} %all-gather.13.cloned.1.call-done) | copy-start | bytes 9437188
  255.6 3.0 copy-start.4
  256.2 3.1 copy-start.3
  256.2 69.4 %collective-permute-start.4 = (bf16[2,3,8,32,512]{4,3,2,0,1:T(8,128)(2,1)S(1)}, bf16[2,3,8,32,512]{4,3,2,0,1:T(8,128)(2,1)S(1)}, u32[]{:S(2)}, u32[]{:S(2)}) collective-permute-start(bf16[2,3,8,32,512]{4,3,2,0,1:T(8,128)(2,1)S(1)} %get-tuple-element.11), channel_id=1, source_target_pairs={{0,4},{4,0},{1,5},{5,1},{2,6},{6,2},{3,7},{7,3},{8,12},{12,8},{9,1... | collective-permute-start | bytes 4718600 | tf_op jit(solution)/shard_map/ppermute | solution.py:27
  274.3 1.1 copy-start.2
  274.9 1.2 copy-start.1
  276.0 1.1 copy-start
  354.6 11.9 %collective-permute-start.5 = (bf16[512,256]{1,0:T(8,128)(2,1)S(1)}, bf16[512,256]{1,0:T(8,128)(2,1)S(1)}, u32[]{:S(2)}, u32[]{:S(2)}) collective-permute-start(bf16[512,256]{1,0:T(8,128)(2,1)S(1)} %fusion.16), channel_id=1, source_target_pairs={{0,4},{4,0},{1,5},{5,1},{2,6},{6,2},{3,7},{7,3},{8,12},{12,8},{9,1... | collective-permute-start | bytes 786440 | tf_op jit(solution)/shard_map/ppermute | solution.py:27
  366.5 0.9 copy-start.7
  366.5 1.0 copy-start.9
Sparse Core Ops, SparseCore 0:
  9.5 25.5 all-gather.8
  36.6 22.8 all-gather.6
  62.3 49.0 all-gather.10
  130.1 29.8 all-gather.12
  162.4 67.9 all-gather.16
  368.5 19.0 all-gather.14
where the time goes:
time: 407 us; the launch traced here: 401 us
  waiting for transfers between devices  257 us (63%)
  local copies, waits for them, and re-layouts  69.1 us (17%)
  other arithmetic  27.3 us (7%)
  matrix products  17.8 us (4%)
  between operations  15.1 us (4%)
  starting transfers between devices  14.5 us (4%)
    ppermute x4, waiting for transfers between devices, partner(): return lax.ppermute(block, axis, route)  157 us
    another operation x23, local copies, waits for them, and re-layouts, cube_block(): jnp.stack([source[:, tap_z:tap_z + planes, tap_y:tap_y + span_y, tap_x:ta...  34.6 us
    all_gather x1, waiting for transfers between devices, local(): portion = lax.all_gather(down_kernel, 'space', axis=1, tiled=True)  32.2 us
    all_gather x1, waiting for transfers between devices, local(): lax.all_gather(fine_state, 'param', axis=3, tiled=True)  21.6 us
    all_gather x1, waiting for transfers between devices, local(): top_full = lax.all_gather(top_stack, 'param', axis=2, tiled=True)  19.1 us
    all_gather x1, waiting for transfers between devices, local(): lax.all_gather(fine_tangent, 'param', axis=3, tiled=True)  18.1 us
    unnamed x39, local copies, waits for them, and re-layouts  12.9 us
    dot_general x18, matrix products, cube_block(): term = jnp.dot(window, weights, preferred_element_type=jnp.float32)  10.5 us
  transfers between devices with their start and end apart: 12, of which 9 were waited for; matrix products, arithmetic and copies ran while one was open for 27% of the time, Pallas kernels for 0%

commit v1 on v0

--- a/solution.py
+++ b/solution.py
@@ -1,7 +1,312 @@
+import functools
+
 import jax
 import jax.numpy as jnp
 from jax import lax
+from jax.experimental import pallas as pl
+from jax.experimental.pallas import tpu as pltpu
 from jax.sharding import PartitionSpec as P
+
+BF16 = jnp.bfloat16
+F32 = jnp.float32
+VMEM = pl.BlockSpec(memory_space=pltpu.VMEM)
+SMEM = pl.BlockSpec(memory_space=pltpu.SMEM)
+
+
+def silu_pair(primal, tangent):
+    sigma = jax.nn.sigmoid(primal)
+    return (primal * sigma, sigma * (1.0 + primal * (1.0 - sigma)) * tangent)
+
+
+def call(kernel, out_shape, args, scratch=(), flops=0, scalars=1):
+    outs = jax.tree.leaves(out_shape)
+    moved = sum(a.size * a.dtype.itemsize for a in (*args, *outs))
+    return pl.pallas_call(
+        kernel,
+        out_shape=out_shape,
+        in_specs=[SMEM] * scalars + [VMEM] * (len(args) - scalars),
+        out_specs=jax.tree.map(lambda _: VMEM, out_shape),
+        scratch_shapes=list(scratch),
+        cost_estimate=pl.CostEstimate(flops=flops, bytes_accessed=moved, transcendentals=0),
+        compiler_params=pltpu.CompilerParams(vmem_limit_bytes=60 * 1024 * 1024),
+    )(*args)
+
+
+def xor_permute(block, axis, mask):
+    count = lax.axis_size(axis)
+    return lax.ppermute(block, axis, [(i, i ^ mask) for i in range(count)])
+
+
+def shift_permute(block, axis, step):
+    count = lax.axis_size(axis)
+    return lax.ppermute(block, axis, [(i, (i + step) % count) for i in range(count)])
+
+
+def gather_space(shard):
+    deep = lax.axis_size("space") // 2
+    column = [(0, shard)]
+    up = down = shard
+    for step in range(1, deep // 2 + 1):
+        up = shift_permute(up, "space", 2)
+        column.append((-step % deep, up))
+        if 2 * step < deep:
+            down = shift_permute(down, "space", -2)
+            column.append((step, down))
+    across = [(far, xor_permute(block, "space", 1)) for far, block in column]
+    return column, across
+
+
+def gather_param(blocks):
+    held = [blocks]
+    mask = lax.axis_size("param") // 2
+    masks = [0]
+    while mask:
+        held += [[xor_permute(b, "param", mask) for b in group] for group in held]
+        masks += [m ^ mask for m in masks]
+        mask //= 2
+    return [held[masks.index(d)] for d in range(len(masks))]
+
+
+def patch_kernel(state_ref, tangent_ref, out_ref, wide):
+    span_y, span_x = state_ref.shape[1] // 2, state_ref.shape[2] // 2
+    cells = span_y * span_x
+    for at, ref in enumerate((state_ref, tangent_ref)):
+        for dz in range(2):
+            wide[...] = ref[dz].astype(F32)
+            for dy in range(2):
+                for dx in range(2):
+                    tap = 4 * dz + 2 * dy + dx
+                    for y in range(span_y):
+                        row = at * cells + y * span_x
+                        out_ref[tap, row : row + span_x, :] = wide[
+                            2 * y + dy, pl.ds(dx, span_x, stride=2), :
+                        ].astype(BF16)
+
+
+def make_down(acts, column, across):
+    n_act, n_col = len(acts), len(column)
+    taps, rows, depth = acts[0].shape
+    _, part, width = column[0][1].shape
+    parts = depth // part
+    deep = n_col
+    half = width // 2
+
+    def kernel(ids_ref, *refs):
+        act_refs = refs[:n_act]
+        shard_refs = refs[n_act : n_act + 2 * n_col]
+        first_ref, same_ref, cross_ref, weight = refs[n_act + 2 * n_col :]
+        p, s = ids_ref[0], ids_ref[1]
+        z, y = s // 2, s % 2
+        for k, (far, _) in enumerate(column):
+            owner = 2 * ((z + far) % deep)
+            weight[owner + y] = shard_refs[k][...]
+            weight[owner + 1 - y] = shard_refs[n_col + k][...]
+        total = None
+        for d in range(n_act):
+            group = (p ^ d) * parts
+            left = jnp.concatenate([act_refs[d][t] for t in range(taps)], axis=1)
+            right = jnp.concatenate(
+                [weight[group + b, t] for t in range(taps) for b in range(parts)], axis=0
+            )
+            term = jnp.dot(left, right, preferred_element_type=F32)
+            total = term if total is None else total + term
+        cells = rows // 2
+        value, slope = silu_pair(total[:cells], total[cells:])
+        first = jnp.concatenate([value, slope], axis=0).astype(BF16)
+        first_ref[...] = first
+        low, high = first[:, :half], first[:, half:]
+        same_ref[...] = jnp.where(y == 0, low, high)
+        cross_ref[...] = jnp.where(y == 0, high, low)
+
+    def run(ids):
+        out = (
+            jax.ShapeDtypeStruct((rows, width), BF16),
+            jax.ShapeDtypeStruct((rows, half), BF16),
+            jax.ShapeDtypeStruct((rows, half), BF16),
+        )
+        return call(
+            kernel,
+            out,
+            (ids, *acts, *[b for _, b in column], *[b for _, b in across]),
+            scratch=[pltpu.VMEM((2 * deep, taps, part, width), BF16)],
+            flops=2 * rows * taps * depth * n_act * width,
+        )
+
+    return run
+
+
+def make_window(pieces, span_y, span_x):
+    flat = [b for pair in pieces for b in pair]
+    rows, depth = flat[0].shape
+    cells = rows // 2
+    planes = len(flat)
+    tall = cells + 2 * span_x
+
+    def kernel(ids_ref, *refs):
+        out_ref = refs[-1]
+        p, y = ids_ref[0], ids_ref[1] % 2
+        edge = jnp.zeros((2, tall, 3 * depth), BF16)
+        out_ref[:, 0] = edge
+        out_ref[:, planes + 1] = edge
+        lane_x = lax.broadcasted_iota(jnp.int32, (cells, depth), 0) % span_x
+        rim = jnp.zeros((span_x, 3 * depth), BF16)
+        for d in range(len(pieces)):
+            for i in range(2):
+                plane = 2 * (p ^ d) + (y if i == 0 else 1 - y) + 1
+                for t in range(2):
+                    here = refs[2 * d + i][t * cells : (t + 1) * cells, :]
+                    wide = here.astype(F32)
+                    left = jnp.where(lane_x == 0, 0.0, pltpu.roll(wide, 1, 0))
+                    right = jnp.where(lane_x == span_x - 1, 0.0, pltpu.roll(wide, cells - 1, 0))
+                    out_ref[t, plane, :span_x, :] = rim
+                    out_ref[t, plane, span_x + cells :, :] = rim
+                    body = jnp.concatenate([left.astype(BF16), here, right.astype(BF16)], axis=1)
+                    out_ref[t, plane, span_x : span_x + cells, :] = body
+
+    def run(ids):
+        out = jax.ShapeDtypeStruct((2, planes + 2, tall, 3 * depth), BF16)
+        return call(kernel, out, (ids, *flat))
+
+    return run
+
+
+def cube_planes(ids, windows, weights, span_x, own, dtype):
+    _, tall_z, tall, deep = windows.shape
+    cells = tall - 2 * span_x
+    width = weights.shape[1]
+    count = (tall_z - 2) // 2
+
+    def kernel(ids_ref, win_ref, weight_ref, *out_refs):
+        s = ids_ref[1]
+        z = s // 2
+        parity = s % 2 if own else 1 - s % 2
+        for e in range(count):
+            plane = 2 * (z ^ e) + parity
+            left = jnp.concatenate(
+                [
+                    jnp.concatenate(
+                        [
+                            win_ref[t, plane + kz, ky * span_x : ky * span_x + cells, :]
+                            for kz in range(3)
+                            for ky in range(3)
+                        ],
+                        axis=1,
+                    )
+                    for t in range(2)
+                ],
+                axis=0,
+            )
+            out_refs[e][...] = jnp.dot(
+                left, weight_ref[...], preferred_element_type=F32
+            ).astype(dtype)
+
+    out = tuple(jax.ShapeDtypeStruct((2 * cells, width), dtype) for _ in range(count))
+    return call(
+        kernel, out, (ids, windows, weights), flops=2 * count * 2 * cells * width * 9 * deep
+    )
+
+
+def make_up(acts, column, across, span_y, span_x):
+    n_act, n_col = len(acts), len(column)
+    rows, depth = acts[0].shape
+    taps, part, width = column[0][1].shape
+    parts = depth // part
+    deep = n_col
+    cells = rows // 2
+
+    def kernel(ids_ref, *refs):
+        act_refs = refs[:n_act]
+        shard_refs = refs[n_act : n_act + 2 * n_col]
+        state_ref, tangent_ref, weight, wide = refs[n_act + 2 * n_col :]
+        p, s = ids_ref[0], ids_ref[1]
+        z, y = s // 2, s % 2
+        for k, (far, _) in enumerate(column):
+            owner = 2 * ((z + far) % deep)
+            weight[owner + y] = shard_refs[k][...]
+            weight[owner + 1 - y] = shard_refs[n_col + k][...]
+        left = jnp.concatenate([act_refs[d][...] for d in range(n_act)], axis=1)
+        for pair in range(taps // 2):
+            right = jnp.concatenate(
+                [
+                    jnp.concatenate(
+                        [weight[(p ^ d) * parts + b, 2 * pair + dx] for dx in range(2)], axis=1
+                    )
+                    for d in range(n_act)
+                    for b in range(parts)
+                ],
+                axis=0,
+            )
+            product = jnp.dot(left, right, preferred_element_type=F32)
+            dz, dy = pair // 2, pair % 2
+            for at, ref in enumerate((state_ref, tangent_ref)):
+                for row in range(span_y):
+                    base = at * cells + row * span_x
+                    for dx in range(2):
+                        wide[row, pl.ds(dx, span_x, stride=2), :] = product[
+                            base : base + span_x, dx * width : (dx + 1) * width
+                        ]
+                for row in range(span_y):
+                    ref[dz, 2 * row + dy] = wide[row].astype(BF16)
+
+    def run(ids):
+        out = jax.ShapeDtypeStruct((2, 2 * span_y, 2 * span_x, width), BF16)
+        return call(
+            kernel,
+            (out, out),
+            (ids, *acts, *[b for _, b in column], *[b for _, b in across]),
+            scratch=[
+                pltpu.VMEM((2 * deep, taps, part, width), BF16),
+                pltpu.VMEM((span_y, 2 * span_x, width), F32),
+            ],
+            flops=2 * rows * n_act * depth * taps * width,
+        )
+
+    return run
+
+
+def stationary(fine_state, fine_tangent, down_weight, conv_weight, up_weight):
+    n_space, n_param = lax.axis_size("space"), lax.axis_size("param")
+    span_y, span_x = fine_state.shape[1] // 2, fine_state.shape[2] // 2
+    cells = span_y * span_x
+    fine_local = fine_state.shape[3]
+    p, s = lax.axis_index("param"), lax.axis_index("space")
+    ids = jnp.stack([p, s]).astype(jnp.int32)
+
+    down_cols = gather_space(down_weight.astype(BF16))
+    patches = call(
+        patch_kernel,
+        jax.ShapeDtypeStruct((8, 2 * cells, fine_local), BF16),
+        (fine_state, fine_tangent),
+        scratch=[pltpu.VMEM((2 * span_y, 2 * span_x, fine_local), F32)],
+        scalars=0,
+    )
+    acts = [group[0] for group in gather_param([patches])]
+    first, same, cross = make_down(acts, *down_cols)(ids)
+
+    def transpose(block, flip):
+        route = []
+        for source in range(n_param * n_space):
+            own_p, own_s = divmod(source, n_space)
+            z, y = divmod(own_s, 2)
+            route.append((source, z * n_space + 2 * own_p + (y ^ flip)))
+        return lax.ppermute(block, ("param", "space"), route)
+
+    pieces = gather_param([transpose(same, 0), transpose(cross, 1)])
+    windows = make_window(pieces, span_y, span_x)(ids)
+    cube = conv_weight.astype(BF16).reshape(-1, conv_weight.shape[2])
+    away = cube_planes(ids, windows, cube, span_x, False, BF16)
+    returned = [xor_permute(block, "space", 1) for block in away]
+    home = cube_planes(ids, windows, cube, span_x, True, F32)
+    sums = [h + r.astype(F32) for h, r in zip(home, returned)]
+    total = sums[0]
+    for e in range(1, len(sums)):
+        total = total + xor_permute(sums[e].astype(BF16), "space", 2 * e).astype(F32)
+    value, slope = silu_pair(total[:cells], total[cells:])
+    second = (jnp.concatenate([value, slope], axis=0) + first.astype(F32)).astype(BF16)
+
+    up_cols = gather_space(up_weight.astype(BF16))
+    tops = [group[0] for group in gather_param([second])]
+    return make_up(tops, *up_cols, span_y, span_x)(ids)
 
 
 def padded(block, sides, width):
@@ -25,11 +330,6 @@
         if high != low and high < count:
             route += [(low, high), (high, low)]
     return lax.ppermute(block, axis, route)
-
-
-def silu_pair(primal, tangent):
-    sigma = jax.nn.sigmoid(primal)
-    return (primal * sigma, sigma * (1.0 + primal * (1.0 - sigma)) * tangent)
 
 
 def cube_block(source, kernel, planes):
@@ -56,7 +356,7 @@
     return result
 
 
-def local(fine_state, fine_tangent, down_weight, conv_weight, up_weight):
+def gathered(fine_state, fine_tangent, down_weight, conv_weight, up_weight):
     planes = fine_state.shape[0] // 2
     span_y = fine_state.shape[1] // 2
     span_x = fine_state.shape[2] // 2
@@ -140,6 +440,13 @@
     return (outputs[0], outputs[1])
 
 
+def local(fine_state, *weights):
+    n_space, n_param = lax.axis_size("space"), lax.axis_size("param")
+    if n_space == 2 * n_param and fine_state.shape[0] == 2:
+        return stationary(fine_state, *weights)
+    return gathered(fine_state, *weights)
+
+
 def solution(mesh):
     in_specs = (
         P("space", None, None, "param"),

time: 407 us -> 183 us (0.45)
  the two profiles are of different devices: /device:TPU:0 before, /device:TPU:16 now
where the time goes in v1:
time: 183 us
  waiting for transfers between devices  99.8 us (55%)
  starting transfers between devices  38.4 us (21%)
  Pallas kernels  32 us (17%)
  other arithmetic  8.97 us (5%)
  local copies, waits for them, and re-layouts  2.83 us (2%)
    ppermute x27, waiting for transfers between devices, xor_permute(): return lax.ppermute(block, axis, [(i, i ^ mask) for i in range(count)])  77.6 us
    pallas_call x6, Pallas kernels, call(): pl.pallas_call(kernel, out_shape=out_shape, in_specs=[SMEM] * scalars + [...  32 us
    ppermute x27, starting transfers between devices, xor_permute(): return lax.ppermute(block, axis, [(i, i ^ mask) for i in range(count)])  25 us
    ppermute x6, waiting for transfers between devices, shift_permute(): lax.ppermute(block, axis, [(i, (i + step) % count) for i in range(count)])  13 us
    ppermute x2, waiting for transfers between devices, transpose(): return lax.ppermute(block, ('param', 'space'), route)  9.27 us
    ppermute x6, starting transfers between devices, shift_permute(): lax.ppermute(block, axis, [(i, (i + step) % count) for i in range(count)])  6.84 us
    ppermute x2, starting transfers between devices, transpose(): return lax.ppermute(block, ('param', 'space'), route)  6.53 us
  transfers between devices with their start and end apart: 35, of which 18 were waited for; matrix products, arithmetic and copies ran while one was open for 5% of the time, Pallas kernels for 11%

profile of v1, /device:TPU:16, one launch (start us, length us, event | category | flops | bytes accessed | tf_op | source)
XLA Modules:
  0.0 182.9 jit_solution(9844732164713313543)
XLA Ops:
  0.6 2.5 %shard_map.68.refs_0_ = bf16[8,512,128]{2,1,0:T(8,128)(2,1)} custom-call(bf16[2,16,64,128]{3,2,1,0:T(8,128)(2,1)} %state_ref.1, bf16[2,16,64,128]{3,2,1,0:T(8,128)(2,1)} %tangent_ref.1), custom_call_target="tpu_custom_call" | custom-call | bytes 2097152 | tf_op jit(solution)/shard_map/pallas_call | solution.py:24
  4.6 23.7 %collective-permute-done.1.refs_2_ = bf16[8,512,128]{2,1,0:T(8,128)(2,1)} collective-permute-done((bf16[8,512,128]{2,1,0:T(8,128)(2,1)}, bf16[8,512,128]{2,1,0:T(8,128)(2,1)}, u32[]{:S(2)}, u32[]{:S(2)}) %collective-permute-start.1) | collective-permute-done | bytes 1048608 | tf_op jit(solution)/shard_map/ppermute | solution.py:37
  29.4 1.6 collective-permute-start.3
  33.0 10.4 %collective-permute-done.3.refs_5_ = bf16[8,64,256]{2,1,0:T(8,128)(2,1)S(1)} collective-permute-done((bf16[8,64,256]{2,1,0:T(8,128)(2,1)S(1)}, bf16[8,64,256]{2,1,0:T(8,128)(2,1)S(1)}, u32[]{:S(2)}, u32[]{:S(2)}) %collective-permute-start.3) | collective-permute-done | bytes 262176 | tf_op jit(solution)/shard_map/ppermute | solution.py:42
  43.4 1.9 %collective-permute-start.5 = (bf16[8,64,256]{2,1,0:T(8,128)(2,1)S(1)}, bf16[8,64,256]{2,1,0:T(8,128)(2,1)}, u32[]{:S(2)}, u32[]{:S(2)}) collective-permute-start(bf16[8,64,256]{2,1,0:T(8,128)(2,1)S(1)} %collective-permute-done.3.refs_5_), channel_id=1, source_target_pairs={{0,2},{1,3},{2,4},{3,5},{4,6},{5,7},{6,0},{7,1},{8,10},{9,11},{10,... | collective-permute-start | bytes 786440 | tf_op jit(solution)/shard_map/ppermute | solution.py:42
  47.4 2.5 %collective-permute-done.5.refs_7_ = bf16[8,64,256]{2,1,0:T(8,128)(2,1)} collective-permute-done((bf16[8,64,256]{2,1,0:T(8,128)(2,1)S(1)}, bf16[8,64,256]{2,1,0:T(8,128)(2,1)}, u32[]{:S(2)}, u32[]{:S(2)}) %collective-permute-start.5) | collective-permute-done | bytes 262176 | tf_op jit(solution)/shard_map/ppermute | solution.py:42
  52.1 2.5 %collective-permute-done.7.refs_9_ = bf16[8,64,256]{2,1,0:T(8,128)(2,1)} collective-permute-done((bf16[8,64,256]{2,1,0:T(8,128)(2,1)S(1)}, bf16[8,64,256]{2,1,0:T(8,128)(2,1)}, u32[]{:S(2)}, u32[]{:S(2)}) %collective-permute-start.7) | collective-permute-done | bytes 262176 | tf_op jit(solution)/shard_map/ppermute | solution.py:37
  54.6 5.6 %collective-permute-done.8.refs_10_ = bf16[8,64,256]{2,1,0:T(8,128)(2,1)} collective-permute-done((bf16[8,64,256]{2,1,0:T(8,128)(2,1)}, bf16[8,64,256]{2,1,0:T(8,128)(2,1)}, u32[]{:S(2)}, u32[]{:S(2)}) %collective-permute-start.8) | collective-permute-done | bytes 262176 | tf_op jit(solution)/shard_map/ppermute | solution.py:37
  60.2 3.0 %collective-permute-done.9.refs_11_ = bf16[8,64,256]{2,1,0:T(8,128)(2,1)} collective-permute-done((bf16[8,64,256]{2,1,0:T(8,128)(2,1)}, bf16[8,64,256]{2,1,0:T(8,128)(2,1)}, u32[]{:S(2)}, u32[]{:S(2)}) %collective-permute-start.9) | collective-permute-done | bytes 262176 | tf_op jit(solution)/shard_map/ppermute | solution.py:37
  63.3 5.0 %shard_map.69 = (bf16[512,256]{1,0:T(8,128)(2,1)}, bf16[512,128]{1,0:T(8,128)(2,1)}, bf16[512,128]{1,0:T(8,128)(2,1)}) custom-call(s32[2]{0:T(128)} %pad_add_fusion.ids_ref, bf16[8,512,128]{2,1,0:T(8,128)(2,1)} %shard_map.68.refs_0_, bf16[8,512,128]{2,1,0:T(8,128)(2,1)} %collective-permute-done.refs_1_, bf16[8,512,128]{2,1,0:T(8,128)(2,1)} %collective-permute-done.1.refs_2_, ...), custom_call_target="tpu_custom_call" | custom-call | flops 1073741824 | bytes 6815752 | tf_op jit(solution)/shard_map/pallas_call | solution.py:24
  68.3 4.1 %collective-permute-start.10 = (bf16[512,128]{1,0:T(8,128)(2,1)}, bf16[512,128]{1,0:T(8,128)(2,1)S(1)}, u32[]{:S(2)}, u32[]{:S(2)}) collective-permute-start(bf16[512,128]{1,0:T(8,128)(2,1)} %get-tuple-element.13), channel_id=1, source_target_pairs={{0,0},{1,1},{2,8},{3,9},{4,16},{5,17},{6,24},{7,25},{8,2},{9,3},{1... | collective-permute-start | bytes 393224 | tf_op jit(solution)/shard_map/ppermute | solution.py:292
  72.4 2.4 %collective-permute-start.11 = (bf16[512,128]{1,0:T(8,128)(2,1)}, bf16[512,128]{1,0:T(8,128)(2,1)S(1)}, u32[]{:S(2)}, u32[]{:S(2)}) collective-permute-start(bf16[512,128]{1,0:T(8,128)(2,1)} %get-tuple-element.14), channel_id=1, source_target_pairs={{0,1},{1,0},{2,9},{3,8},{4,17},{5,16},{6,25},{7,24},{8,3},{9,2},{1... | collective-permute-start | bytes 393224 | tf_op jit(solution)/shard_map/ppermute | solution.py:292
  74.9 6.5 %collective-permute-done.10.refs_0_ = bf16[512,128]{1,0:T(8,128)(2,1)S(1)} collective-permute-done((bf16[512,128]{1,0:T(8,128)(2,1)}, bf16[512,128]{1,0:T(8,128)(2,1)S(1)}, u32[]{:S(2)}, u32[]{:S(2)}) %collective-permute-start.10) | collective-permute-done | bytes 131104 | tf_op jit(solution)/shard_map/ppermute | solution.py:292
  81.3 2.8 %collective-permute-done.11.refs_1_ = bf16[512,128]{1,0:T(8,128)(2,1)S(1)} collective-permute-done((bf16[512,128]{1,0:T(8,128)(2,1)}, bf16[512,128]{1,0:T(8,128)(2,1)S(1)}, u32[]{:S(2)}, u32[]{:S(2)}) %collective-permute-start.11) | collective-permute-done | bytes 131104 | tf_op jit(solution)/shard_map/ppermute | solution.py:292
  85.4 2.0 %collective-permute-done.14.refs_4_ = bf16[512,128]{1,0:T(8,128)(2,1)S(1)} collective-permute-done((bf16[512,128]{1,0:T(8,128)(2,1)S(1)}, bf16[512,128]{1,0:T(8,128)(2,1)S(1)}, u32[]{:S(2)}, u32[]{:S(2)}) %collective-permute-start.14) | collective-permute-done | bytes 131104 | tf_op jit(solution)/shard_map/ppermute | solution.py:37
  87.4 2.9 %collective-permute-done.15.refs_5_ = bf16[512,128]{1,0:T(8,128)(2,1)S(1)} collective-permute-done((bf16[512,128]{1,0:T(8,128)(2,1)S(1)}, bf16[512,128]{1,0:T(8,128)(2,1)S(1)}, u32[]{:S(2)}, u32[]{:S(2)}) %collective-permute-start.15) | collective-permute-done | bytes 131104 | tf_op jit(solution)/shard_map/ppermute | solution.py:37
  94.5 4.5 %shard_map.70.win_ref = bf16[2,10,320,384]{3,2,1,0:T(8,128)(2,1)} custom-call(s32[2]{0:T(128)} %pad_add_fusion.ids_ref, bf16[512,128]{1,0:T(8,128)(2,1)} %copy-done.7, bf16[512,128]{1,0:T(8,128)(2,1)} %copy-done.8, bf16[512,128]{1,0:T(8,128)(2,1)} %copy-done.11, bf16[512,128]{1,0:T(8,128)(2,1)} %copy-done.12, bf16[512,128]{1,0:T(8,128)(2,1)} %copy-done.9, ...), custom_call_target="tpu_custom_call" | custom-call | bytes 5963784 | tf_op jit(solution)/shard_map/pallas_call | solution.py:24
  98.9 7.7 %shard_map.72 = (bf16[512,256]{1,0:T(8,128)(2,1)}, bf16[512,256]{1,0:T(8,128)(2,1)}, bf16[512,256]{1,0:T(8,128)(2,1)}, bf16[512,256]{1,0:T(8,128)(2,1)}) custom-call(s32[2]{0:T(128)} %pad_add_fusion.ids_ref, bf16[2,10,320,384]{3,2,1,0:T(8,128)(2,1)} %shard_map.70.win_ref, bf16[3456,256]{1,0:T(8,128)(2,1)} %bitcast.3), custom_call_target="tpu_custom_call" | custom-call | flops 3623878656 | bytes 7733256 | tf_op jit(solution)/shard_map/pallas_call | solution.py:24
  108.7 8.0 %shard_map.71 = (f32[512,256]{1,0:T(8,128)}, f32[512,256]{1,0:T(8,128)}, f32[512,256]{1,0:T(8,128)}, f32[512,256]{1,0:T(8,128)}) custom-call(s32[2]{0:T(128)} %pad_add_fusion.ids_ref, bf16[2,10,320,384]{3,2,1,0:T(8,128)(2,1)} %shard_map.70.win_ref, bf16[3456,256]{1,0:T(8,128)(2,1)} %bitcast.4), custom_call_target="tpu_custom_call" | custom-call | flops 3623878656 | bytes 8781832 | tf_op jit(solution)/shard_map/pallas_call | solution.py:24
  119.8 3.9 %collective-permute-start.20 = (bf16[512,256]{1,0:T(8,128)(2,1)S(1)}, bf16[512,256]{1,0:T(8,128)(2,1)S(1)}, u32[]{:S(2)}, u32[]{:S(2)}) collective-permute-start(bf16[512,256]{1,0:T(8,128)(2,1)S(1)} %add_convert_fusion.2), channel_id=1, source_target_pairs={{0,2},{1,3},{2,0},{3,1},{4,6},{5,7},{6,4},{7,5},{8,10},{9,11},{10,... | collective-permute-start | bytes 786440 | tf_op jit(solution)/shard_map/ppermute | solution.py:37
  128.4 2.1 %collective-permute-start.24 = (bf16[512,256]{1,0:T(8,128)(2,1)S(1)}, bf16[512,256]{1,0:T(8,128)(2,1)S(1)}, u32[]{:S(2)}, u32[]{:S(2)}) collective-permute-start(bf16[512,256]{1,0:T(8,128)(2,1)S(1)} %add_convert_fusion), channel_id=1, source_target_pairs={{0,6},{1,7},{2,4},{3,5},{4,2},{5,3},{6,0},{7,1},{8,14},{9,15},{10,... | collective-permute-start | bytes 786440 | tf_op jit(solution)/shard_map/ppermute | solution.py:37
  130.5 1.8 collective-permute-done.18
  133.7 2.7 %collective-permute-start.30 = (bf16[8,128,128]{2,1,0:T(8,128)(2,1)}, bf16[8,128,128]{2,1,0:T(8,128)(2,1)S(1)}, u32[]{:S(2)}, u32[]{:S(2)}) collective-permute-start(bf16[8,128,128]{2,1,0:T(8,128)(2,1)} %collective-permute-done.28.refs_5_), channel_id=1, source_target_pairs={{0,2},{1,3},{2,4},{3,5},{4,6},{5,7},{6,0},{7,1},{8,10},{9,11},{10,... | collective-permute-start | bytes 786440 | tf_op jit(solution)/shard_map/ppermute | solution.py:42
  136.5 7.3 %collective-permute-done.22 = bf16[512,256]{1,0:T(8,128)(2,1)S(1)} collective-permute-done((bf16[512,256]{1,0:T(8,128)(2,1)S(1)}, bf16[512,256]{1,0:T(8,128)(2,1)S(1)}, u32[]{:S(2)}, u32[]{:S(2)}) %collective-permute-start.22) | collective-permute-done | bytes 262176 | tf_op jit(solution)/shard_map/ppermute | solution.py:37
  143.7 12.8 %collective-permute-done.24 = bf16[512,256]{1,0:T(8,128)(2,1)S(1)} collective-permute-done((bf16[512,256]{1,0:T(8,128)(2,1)S(1)}, bf16[512,256]{1,0:T(8,128)(2,1)S(1)}, u32[]{:S(2)}, u32[]{:S(2)}) %collective-permute-start.24) | collective-permute-done | bytes 262176 | tf_op jit(solution)/shard_map/ppermute | solution.py:37
  157.9 2.1 %collective-permute-start.26 = (bf16[512,256]{1,0:T(8,128)(2,1)S(1)}, bf16[512,256]{1,0:T(8,128)(2,1)S(1)}, u32[]{:S(2)}, u32[]{:S(2)}) collective-permute-start(bf16[512,256]{1,0:T(8,128)(2,1)S(1)} %fusion.refs_0_), channel_id=1, source_target_pairs={{0,16},{8,24},{16,0},{24,8},{1,17},{9,25},{17,1},{25,9},{2,18},{10... | collective-permute-start | bytes 786440 | tf_op jit(solution)/shard_map/ppermute | solution.py:37
  160.6 1.5 collective-permute-start.33
  162.6 1.8 collective-permute-done.26.refs_2_
  164.4 5.0 %collective-permute-done.32.refs_9_ = bf16[8,128,128]{2,1,0:T(8,128)(2,1)S(1)} collective-permute-done((bf16[8,128,128]{2,1,0:T(8,128)(2,1)}, bf16[8,128,128]{2,1,0:T(8,128)(2,1)S(1)}, u32[]{:S(2)}, u32[]{:S(2)}) %collective-permute-start.32) | collective-permute-done | bytes 262176 | tf_op jit(solution)/shard_map/ppermute | solution.py:37
  169.5 4.8 %collective-permute-done.33.refs_10_ = bf16[8,128,128]{2,1,0:T(8,128)(2,1)S(1)} collective-permute-done((bf16[8,128,128]{2,1,0:T(8,128)(2,1)S(1)}, bf16[8,128,128]{2,1,0:T(8,128)(2,1)S(1)}, u32[]{:S(2)}, u32[]{:S(2)}) %collective-permute-start.33) | collective-permute-done | bytes 262176 | tf_op jit(solution)/shard_map/ppermute | solution.py:37
  174.2 2.8 %collective-permute-done.34.refs_11_ = bf16[8,128,128]{2,1,0:T(8,128)(2,1)S(1)} collective-permute-done((bf16[8,128,128]{2,1,0:T(8,128)(2,1)S(1)}, bf16[8,128,128]{2,1,0:T(8,128)(2,1)S(1)}, u32[]{:S(2)}, u32[]{:S(2)}) %collective-permute-start.34) | collective-permute-done | bytes 262176 | tf_op jit(solution)/shard_map/ppermute | solution.py:37
  178.6 4.4 %shard_map.73 = (bf16[2,16,64,128]{3,2,1,0:T(8,128)(2,1)}, bf16[2,16,64,128]{3,2,1,0:T(8,128)(2,1)}) custom-call(s32[2]{0:T(128)} %pad_add_fusion.ids_ref, bf16[512,256]{1,0:T(8,128)(2,1)} %copy-done.6, bf16[512,256]{1,0:T(8,128)(2,1)} %copy-done.23, bf16[512,256]{1,0:T(8,128)(2,1)} %copy-done.18, bf16[512,256]{1,0:T(8,128)(2,1)} %copy-done.24, ...), custom_call_target="tpu_custom_call" | custom-call | flops 1073741824 | bytes 4194312 | tf_op jit(solution)/shard_map/pallas_call | solution.py:24
  (104 shorter events, 29.3 us)
Async XLA Ops:
  3.1 25.2 %collective-permute-start.1 = (bf16[8,512,128]{2,1,0:T(8,128)(2,1)}, bf16[8,512,128]{2,1,0:T(8,128)(2,1)}, u32[]{:S(2)}, u32[]{:S(2)}) collective-permute-start(bf16[8,512,128]{2,1,0:T(8,128)(2,1)} %shard_map.68.refs_0_), channel_id=1, source_target_pairs={{0,16},{8,24},{16,0},{24,8},{1,17},{9,25},{17,1},{25,9},{2,18},{10... | collective-permute-start | bytes 3145736 | tf_op jit(solution)/shard_map/ppermute | solution.py:37
  4.6 58.7 %collective-permute-start = (bf16[8,512,128]{2,1,0:T(8,128)(2,1)}, bf16[8,512,128]{2,1,0:T(8,128)(2,1)}, u32[]{:S(2)}, u32[]{:S(2)}) collective-permute-start(bf16[8,512,128]{2,1,0:T(8,128)(2,1)} %shard_map.68.refs_0_), channel_id=1, source_target_pairs={{0,8},{8,0},{16,24},{24,16},{1,9},{9,1},{17,25},{25,17},{2,10},{10... | collective-permute-start | bytes 3145736 | tf_op jit(solution)/shard_map/ppermute | solution.py:37
  28.3 34.9 %collective-permute-start.2 = (bf16[8,512,128]{2,1,0:T(8,128)(2,1)}, bf16[8,512,128]{2,1,0:T(8,128)(2,1)}, u32[]{:S(2)}, u32[]{:S(2)}) collective-permute-start(bf16[8,512,128]{2,1,0:T(8,128)(2,1)} %collective-permute-done.1.refs_2_), channel_id=1, source_target_pairs={{0,8},{8,0},{16,24},{24,16},{1,9},{9,1},{17,25},{25,17},{2,10},{10... | collective-permute-start | bytes 3145736 | tf_op jit(solution)/shard_map/ppermute | solution.py:37
  29.4 14.0 %collective-permute-start.3 = (bf16[8,64,256]{2,1,0:T(8,128)(2,1)S(1)}, bf16[8,64,256]{2,1,0:T(8,128)(2,1)S(1)}, u32[]{:S(2)}, u32[]{:S(2)}) collective-permute-start(bf16[8,64,256]{2,1,0:T(8,128)(2,1)S(1)} %convert_element_type.45.refs_4_), channel_id=1, source_target_pairs={{0,2},{1,3},{2,4},{3,5},{4,6},{5,7},{6,0},{7,1},{8,10},{9,11},{10,... | collective-permute-start | bytes 786440 | tf_op jit(solution)/shard_map/ppermute | solution.py:42
  31.0 14.3 %collective-permute-start.4 = (bf16[8,64,256]{2,1,0:T(8,128)(2,1)S(1)}, bf16[8,64,256]{2,1,0:T(8,128)(2,1)}, u32[]{:S(2)}, u32[]{:S(2)}) collective-permute-start(bf16[8,64,256]{2,1,0:T(8,128)(2,1)S(1)} %convert_element_type.45.refs_4_), channel_id=1, source_target_pairs={{0,6},{1,7},{2,0},{3,1},{4,2},{5,3},{6,4},{7,5},{8,14},{9,15},{10,... | collective-permute-start | bytes 786440 | tf_op jit(solution)/shard_map/ppermute | solution.py:42
  31.5 15.4 %collective-permute-start.6 = (bf16[8,64,256]{2,1,0:T(8,128)(2,1)S(1)}, bf16[8,64,256]{2,1,0:T(8,128)(2,1)S(1)}, u32[]{:S(2)}, u32[]{:S(2)}) collective-permute-start(bf16[8,64,256]{2,1,0:T(8,128)(2,1)S(1)} %convert_element_type.45.refs_4_), channel_id=1, source_target_pairs={{0,1},{1,0},{2,3},{3,2},{4,5},{5,4},{6,7},{7,6},{8,9},{9,8},{10,11... | collective-permute-start | bytes 786440 | tf_op jit(solution)/shard_map/ppermute | solution.py:37
  43.4 6.5 %collective-permute-start.5 = (bf16[8,64,256]{2,1,0:T(8,128)(2,1)S(1)}, bf16[8,64,256]{2,1,0:T(8,128)(2,1)}, u32[]{:S(2)}, u32[]{:S(2)}) collective-permute-start(bf16[8,64,256]{2,1,0:T(8,128)(2,1)S(1)} %collective-permute-done.3.refs_5_), channel_id=1, source_target_pairs={{0,2},{1,3},{2,4},{3,5},{4,6},{5,7},{6,0},{7,1},{8,10},{9,11},{10,... | collective-permute-start | bytes 786440 | tf_op jit(solution)/shard_map/ppermute | solution.py:42
  45.3 9.3 %collective-permute-start.7 = (bf16[8,64,256]{2,1,0:T(8,128)(2,1)S(1)}, bf16[8,64,256]{2,1,0:T(8,128)(2,1)}, u32[]{:S(2)}, u32[]{:S(2)}) collective-permute-start(bf16[8,64,256]{2,1,0:T(8,128)(2,1)S(1)} %collective-permute-done.3.refs_5_), channel_id=1, source_target_pairs={{0,1},{1,0},{2,3},{3,2},{4,5},{5,4},{6,7},{7,6},{8,9},{9,8},{10,11... | collective-permute-start | bytes 786440 | tf_op jit(solution)/shard_map/ppermute | solution.py:37
  46.9 13.4 %collective-permute-start.8 = (bf16[8,64,256]{2,1,0:T(8,128)(2,1)}, bf16[8,64,256]{2,1,0:T(8,128)(2,1)}, u32[]{:S(2)}, u32[]{:S(2)}) collective-permute-start(bf16[8,64,256]{2,1,0:T(8,128)(2,1)} %collective-permute-done.4.refs_6_), channel_id=1, source_target_pairs={{0,1},{1,0},{2,3},{3,2},{4,5},{5,4},{6,7},{7,6},{8,9},{9,8},{10,11... | collective-permute-start | bytes 786440 | tf_op jit(solution)/shard_map/ppermute | solution.py:37
  49.9 13.4 %collective-permute-start.9 = (bf16[8,64,256]{2,1,0:T(8,128)(2,1)}, bf16[8,64,256]{2,1,0:T(8,128)(2,1)}, u32[]{:S(2)}, u32[]{:S(2)}) collective-permute-start(bf16[8,64,256]{2,1,0:T(8,128)(2,1)} %collective-permute-done.5.refs_7_), channel_id=1, source_target_pairs={{0,1},{1,0},{2,3},{3,2},{4,5},{5,4},{6,7},{7,6},{8,9},{9,8},{10,11... | collective-permute-start | bytes 786440 | tf_op jit(solution)/shard_map/ppermute | solution.py:37
  68.3 13.0 %collective-permute-start.10 = (bf16[512,128]{1,0:T(8,128)(2,1)}, bf16[512,128]{1,0:T(8,128)(2,1)S(1)}, u32[]{:S(2)}, u32[]{:S(2)}) collective-permute-start(bf16[512,128]{1,0:T(8,128)(2,1)} %get-tuple-element.13), channel_id=1, source_target_pairs={{0,0},{1,1},{2,8},{3,9},{4,16},{5,17},{6,24},{7,25},{8,2},{9,3},{1... | collective-permute-start | bytes 393224 | tf_op jit(solution)/shard_map/ppermute | solution.py:292
  72.4 11.7 %collective-permute-start.11 = (bf16[512,128]{1,0:T(8,128)(2,1)}, bf16[512,128]{1,0:T(8,128)(2,1)S(1)}, u32[]{:S(2)}, u32[]{:S(2)}) collective-permute-start(bf16[512,128]{1,0:T(8,128)(2,1)} %get-tuple-element.14), channel_id=1, source_target_pairs={{0,1},{1,0},{2,9},{3,8},{4,17},{5,16},{6,25},{7,24},{8,3},{9,2},{1... | collective-permute-start | bytes 393224 | tf_op jit(solution)/shard_map/ppermute | solution.py:292
  84.1 6.2 %collective-permute-start.15 = (bf16[512,128]{1,0:T(8,128)(2,1)S(1)}, bf16[512,128]{1,0:T(8,128)(2,1)S(1)}, u32[]{:S(2)}, u32[]{:S(2)}) collective-permute-start(bf16[512,128]{1,0:T(8,128)(2,1)S(1)} %collective-permute-done.11.refs_1_), channel_id=1, source_target_pairs={{0,16},{8,24},{16,0},{24,8},{1,17},{9,25},{17,1},{25,9},{2,18},{10... | collective-permute-start | bytes 393224 | tf_op jit(solution)/shard_map/ppermute | solution.py:37
  84.1 8.9 %collective-permute-start.12 = (bf16[512,128]{1,0:T(8,128)(2,1)S(1)}, bf16[512,128]{1,0:T(8,128)(2,1)S(1)}, u32[]{:S(2)}, u32[]{:S(2)}) collective-permute-start(bf16[512,128]{1,0:T(8,128)(2,1)S(1)} %collective-permute-done.10.refs_0_), channel_id=1, source_target_pairs={{0,8},{8,0},{16,24},{24,16},{1,9},{9,1},{17,25},{25,17},{2,10},{10... | collective-permute-start | bytes 393224 | tf_op jit(solution)/shard_map/ppermute | solution.py:37
  85.3 7.8 %collective-permute-start.13 = (bf16[512,128]{1,0:T(8,128)(2,1)S(1)}, bf16[512,128]{1,0:T(8,128)(2,1)S(1)}, u32[]{:S(2)}, u32[]{:S(2)}) collective-permute-start(bf16[512,128]{1,0:T(8,128)(2,1)S(1)} %collective-permute-done.11.refs_1_), channel_id=1, source_target_pairs={{0,8},{8,0},{16,24},{24,16},{1,9},{9,1},{17,25},{25,17},{2,10},{10... | collective-permute-start | bytes 393224 | tf_op jit(solution)/shard_map/ppermute | solution.py:37
  91.5 38.9 %collective-permute-start.28 = (bf16[8,128,128]{2,1,0:T(8,128)(2,1)S(1)}, bf16[8,128,128]{2,1,0:T(8,128)(2,1)}, u32[]{:S(2)}, u32[]{:S(2)}) collective-permute-start(bf16[8,128,128]{2,1,0:T(8,128)(2,1)S(1)} %convert_element_type.59.refs_4_), channel_id=1, source_target_pairs={{0,2},{1,3},{2,4},{3,5},{4,6},{5,7},{6,0},{7,1},{8,10},{9,11},{10,... | collective-permute-start | bytes 786440 | tf_op jit(solution)/shard_map/ppermute | solution.py:42
  106.6 12.0 %collective-permute-start.19 = (bf16[512,256]{1,0:T(8,128)(2,1)}, bf16[512,256]{1,0:T(8,128)(2,1)S(1)}, u32[]{:S(2)}, u32[]{:S(2)}) collective-permute-start(bf16[512,256]{1,0:T(8,128)(2,1)} %get-tuple-element.18), channel_id=1, source_target_pairs={{0,1},{1,0},{2,3},{3,2},{4,5},{5,4},{6,7},{7,6},{8,9},{9,8},{10,11... | collective-permute-start | bytes 786440 | tf_op jit(solution)/shard_map/ppermute | solution.py:37
  108.0 15.7 %collective-permute-start.21 = (bf16[512,256]{1,0:T(8,128)(2,1)}, bf16[512,256]{1,0:T(8,128)(2,1)S(1)}, u32[]{:S(2)}, u32[]{:S(2)}) collective-permute-start(bf16[512,256]{1,0:T(8,128)(2,1)} %get-tuple-element.20), channel_id=1, source_target_pairs={{0,1},{1,0},{2,3},{3,2},{4,5},{5,4},{6,7},{7,6},{8,9},{9,8},{10,11... | collective-permute-start | bytes 786440 | tf_op jit(solution)/shard_map/ppermute | solution.py:37
  116.6 10.6 %collective-permute-start.23 = (bf16[512,256]{1,0:T(8,128)(2,1)S(1)}, bf16[512,256]{1,0:T(8,128)(2,1)S(1)}, u32[]{:S(2)}, u32[]{:S(2)}) collective-permute-start(bf16[512,256]{1,0:T(8,128)(2,1)S(1)} %copy-done.21), channel_id=1, source_target_pairs={{0,1},{1,0},{2,3},{3,2},{4,5},{5,4},{6,7},{7,6},{8,9},{9,8},{10,11... | collective-permute-start | bytes 786440 | tf_op jit(solution)/shard_map/ppermute | solution.py:37
  118.0 14.3 %collective-permute-start.18 = (bf16[512,256]{1,0:T(8,128)(2,1)S(1)}, bf16[512,256]{1,0:T(8,128)(2,1)S(1)}, u32[]{:S(2)}, u32[]{:S(2)}) collective-permute-start(bf16[512,256]{1,0:T(8,128)(2,1)S(1)} %copy-done.17), channel_id=1, source_target_pairs={{0,1},{1,0},{2,3},{3,2},{4,5},{5,4},{6,7},{7,6},{8,9},{9,8},{10,11... | collective-permute-start | bytes 786440 | tf_op jit(solution)/shard_map/ppermute | solution.py:37
  119.8 14.0 %collective-permute-start.20 = (bf16[512,256]{1,0:T(8,128)(2,1)S(1)}, bf16[512,256]{1,0:T(8,128)(2,1)S(1)}, u32[]{:S(2)}, u32[]{:S(2)}) collective-permute-start(bf16[512,256]{1,0:T(8,128)(2,1)S(1)} %add_convert_fusion.2), channel_id=1, source_target_pairs={{0,2},{1,3},{2,0},{3,1},{4,6},{5,7},{6,4},{7,5},{8,10},{9,11},{10,... | collective-permute-start | bytes 786440 | tf_op jit(solution)/shard_map/ppermute | solution.py:37
  124.8 18.9 %collective-permute-start.22 = (bf16[512,256]{1,0:T(8,128)(2,1)S(1)}, bf16[512,256]{1,0:T(8,128)(2,1)S(1)}, u32[]{:S(2)}, u32[]{:S(2)}) collective-permute-start(bf16[512,256]{1,0:T(8,128)(2,1)S(1)} %add_convert_fusion.1), channel_id=1, source_target_pairs={{0,4},{1,5},{2,6},{3,7},{4,0},{5,1},{6,2},{7,3},{8,12},{9,13},{10,... | collective-permute-start | bytes 786440 | tf_op jit(solution)/shard_map/ppermute | solution.py:37
  128.4 28.2 %collective-permute-start.24 = (bf16[512,256]{1,0:T(8,128)(2,1)S(1)}, bf16[512,256]{1,0:T(8,128)(2,1)S(1)}, u32[]{:S(2)}, u32[]{:S(2)}) collective-permute-start(bf16[512,256]{1,0:T(8,128)(2,1)S(1)} %add_convert_fusion), channel_id=1, source_target_pairs={{0,6},{1,7},{2,4},{3,5},{4,2},{5,3},{6,0},{7,1},{8,14},{9,15},{10,... | collective-permute-start | bytes 786440 | tf_op jit(solution)/shard_map/ppermute | solution.py:37
  130.4 30.1 %collective-permute-start.29 = (bf16[8,128,128]{2,1,0:T(8,128)(2,1)S(1)}, bf16[8,128,128]{2,1,0:T(8,128)(2,1)S(1)}, u32[]{:S(2)}, u32[]{:S(2)}) collective-permute-start(bf16[8,128,128]{2,1,0:T(8,128)(2,1)S(1)} %convert_element_type.59.refs_4_), channel_id=1, source_target_pairs={{0,6},{1,7},{2,0},{3,1},{4,2},{5,3},{6,4},{7,5},{8,14},{9,15},{10,... | collective-permute-start | bytes 786440 | tf_op jit(solution)/shard_map/ppermute | solution.py:42
  132.3 30.3 %collective-permute-start.31 = (bf16[8,128,128]{2,1,0:T(8,128)(2,1)S(1)}, bf16[8,128,128]{2,1,0:T(8,128)(2,1)S(1)}, u32[]{:S(2)}, u32[]{:S(2)}) collective-permute-start(bf16[8,128,128]{2,1,0:T(8,128)(2,1)S(1)} %convert_element_type.59.refs_4_), channel_id=1, source_target_pairs={{0,1},{1,0},{2,3},{3,2},{4,5},{5,4},{6,7},{7,6},{8,9},{9,8},{10,11... | collective-permute-start | bytes 786440 | tf_op jit(solution)/shard_map/ppermute | solution.py:37
  133.7 28.4 %collective-permute-start.30 = (bf16[8,128,128]{2,1,0:T(8,128)(2,1)}, bf16[8,128,128]{2,1,0:T(8,128)(2,1)S(1)}, u32[]{:S(2)}, u32[]{:S(2)}) collective-permute-start(bf16[8,128,128]{2,1,0:T(8,128)(2,1)} %collective-permute-done.28.refs_5_), channel_id=1, source_target_pairs={{0,2},{1,3},{2,4},{3,5},{4,6},{5,7},{6,0},{7,1},{8,10},{9,11},{10,... | collective-permute-start | bytes 786440 | tf_op jit(solution)/shard_map/ppermute | solution.py:42
  157.9 6.5 %collective-permute-start.26 = (bf16[512,256]{1,0:T(8,128)(2,1)S(1)}, bf16[512,256]{1,0:T(8,128)(2,1)S(1)}, u32[]{:S(2)}, u32[]{:S(2)}) collective-permute-start(bf16[512,256]{1,0:T(8,128)(2,1)S(1)} %fusion.refs_0_), channel_id=1, source_target_pairs={{0,16},{8,24},{16,0},{24,8},{1,17},{9,25},{17,1},{25,9},{2,18},{10... | collective-permute-start | bytes 786440 | tf_op jit(solution)/shard_map/ppermute | solution.py:37
  160.1 9.4 %collective-permute-start.32 = (bf16[8,128,128]{2,1,0:T(8,128)(2,1)}, bf16[8,128,128]{2,1,0:T(8,128)(2,1)S(1)}, u32[]{:S(2)}, u32[]{:S(2)}) collective-permute-start(bf16[8,128,128]{2,1,0:T(8,128)(2,1)} %collective-permute-done.28.refs_5_), channel_id=1, source_target_pairs={{0,1},{1,0},{2,3},{3,2},{4,5},{5,4},{6,7},{7,6},{8,9},{9,8},{10,11... | collective-permute-start | bytes 786440 | tf_op jit(solution)/shard_map/ppermute | solution.py:37
  160.6 13.6 %collective-permute-start.33 = (bf16[8,128,128]{2,1,0:T(8,128)(2,1)S(1)}, bf16[8,128,128]{2,1,0:T(8,128)(2,1)S(1)}, u32[]{:S(2)}, u32[]{:S(2)}) collective-permute-start(bf16[8,128,128]{2,1,0:T(8,128)(2,1)S(1)} %collective-permute-done.29.refs_6_), channel_id=1, source_target_pairs={{0,1},{1,0},{2,3},{3,2},{4,5},{5,4},{6,7},{7,6},{8,9},{9,8},{10,11... | collective-permute-start | bytes 786440 | tf_op jit(solution)/shard_map/ppermute | solution.py:37
  162.1 14.9 %collective-permute-start.34 = (bf16[8,128,128]{2,1,0:T(8,128)(2,1)S(1)}, bf16[8,128,128]{2,1,0:T(8,128)(2,1)S(1)}, u32[]{:S(2)}, u32[]{:S(2)}) collective-permute-start(bf16[8,128,128]{2,1,0:T(8,128)(2,1)S(1)} %collective-permute-done.30.refs_7_), channel_id=1, source_target_pairs={{0,1},{1,0},{2,3},{3,2},{4,5},{5,4},{6,7},{7,6},{8,9},{9,8},{10,11... | collective-permute-start | bytes 786440 | tf_op jit(solution)/shard_map/ppermute | solution.py:37
  162.6 14.4 %collective-permute-start.25 = (bf16[512,256]{1,0:T(8,128)(2,1)S(1)}, bf16[512,256]{1,0:T(8,128)(2,1)S(1)}, u32[]{:S(2)}, u32[]{:S(2)}) collective-permute-start(bf16[512,256]{1,0:T(8,128)(2,1)S(1)} %fusion.refs_0_), channel_id=1, source_target_pairs={{0,8},{8,0},{16,24},{24,16},{1,9},{9,1},{17,25},{25,17},{2,10},{10... | collective-permute-start | bytes 786440 | tf_op jit(solution)/shard_map/ppermute | solution.py:37
  164.4 12.6 %collective-permute-start.27 = (bf16[512,256]{1,0:T(8,128)(2,1)S(1)}, bf16[512,256]{1,0:T(8,128)(2,1)S(1)}, u32[]{:S(2)}, u32[]{:S(2)}) collective-permute-start(bf16[512,256]{1,0:T(8,128)(2,1)S(1)} %collective-permute-done.26.refs_2_), channel_id=1, source_target_pairs={{0,8},{8,0},{16,24},{24,16},{1,9},{9,1},{17,25},{25,17},{2,10},{10... | collective-permute-start | bytes 786440 | tf_op jit(solution)/shard_map/ppermute | solution.py:37
  (28 other events, 337.3 us)
